TPU v7x, 128 devices: a whole 4x4x4 slice. The times are simulated.
128 devices in a mesh: lat: 16 (over x, z_lo, core), lon: 8 (over z_hi, y).
Axes of the slice: x: 4, y: 4, z: 4 (z_hi: 2, z_lo: 2; z = z_hi * 2 + z_lo), core: 2. Of those that a mesh axis runs over, the one named last changes fastest.
Arguments:
- x_tiles: bfloat16 [8, 64, 77, 256], P('lon', 'lat'), may hold values from -6 to 6
- tile_pos: int32 [8, 64], P('lon', 'lat'), may hold values from 0 to 511, as said below
- valid_rows: int32 [8, 64], P('lon', 'lat'), may hold values from 1 to 16
- stem_w: bfloat16 [77, 200], replicated, may hold values from -0.625 to 0.625
- dw_kernel: float32 [200, 49], replicated, may hold values from -0.875 to 0.875
- norm_gain: float32 [200], replicated, may hold values from 0.1 to 1.9
- w_in: bfloat16 [200, 800], replicated, may hold values from -0.4375 to 0.4375
- w_out: bfloat16 [800, 200], replicated, may hold values from -0.21875 to 0.21875
- cotangent: bfloat16 [8, 64, 200, 256], P('lon', 'lat'), may hold values from -3072 to 3072
Outputs:
- out_tiles: bfloat16 [8, 64, 200, 256], P('lon', 'lat')
- grad_w_in: float32 [200, 800], replicated
- grad_w_out: float32 [800, 200], replicated
- grad_kernel: float32 [200, 49], replicated
- grad_gain: float32 [200], replicated
Inputs may be any that keep to these rules, and one draw needn't show every extreme that they name: `tile_pos`: in each sector the places are distinct; in the order of place, the r-th active tile of a sector is held by lat index r % 16. At most 2 tiles of one device lie in one band block of 32 tiles, and this is reached; some band block is fully active in every sector.
All inputs are finite; a program needn't handle non-finite values.
Results may differ from a plain program's by a relative error of at most 0.0075.
Values may be sent and summed in bfloat16 or wider, within the bound.
No kernel may reach another device: no remote copies, remote signals or barrier semaphores. Data moves between devices by JAX's collectives and lax.ppermute only.
A program may use at most 128 MiB of HBM per device.

v0:
```python
import jax
import jax.numpy as jnp
from jax import lax
from jax.sharding import PartitionSpec as P

C = 200
CIN = 77
KW = 7
TS = 16
BH = 64
BW = 128
K_TILES = 32


def extended(block, sides, width, periodic):
    for axis, dim in sides:
        count = lax.axis_size(axis)
        forward = [(i, i + 1) for i in range(count - 1)]
        if periodic:
            forward.append((count - 1, 0))
        backward = [(target, source) for source, target in forward]
        low = lax.ppermute(
            lax.slice_in_dim(block, block.shape[dim] - width, None, axis=dim), axis, forward
        )
        high = lax.ppermute(lax.slice_in_dim(block, 0, width, axis=dim), axis, backward)
        block = jnp.concatenate([low, block, high], axis=dim)
    return block


def gelu_tanh(value):
    return jax.nn.gelu(value, approximate=True)


def tiles_to_block(tiles):
    chan = tiles.shape[1]
    shaped = tiles.reshape(BH // TS, BW // TS, chan, TS, TS)
    return shaped.transpose(2, 0, 3, 1, 4).reshape(chan, BH, BW)


def block_to_tiles(block):
    chan = block.shape[0]
    shaped = block.reshape(chan, BH // TS, TS, BW // TS, TS)
    return shaped.transpose(1, 3, 0, 2, 4).reshape(K_TILES, chan, TS * TS)


def select_rows(onehot, tiles):
    return jnp.einsum("qa,acp->qcp", onehot, tiles, preferred_element_type=jnp.float32).astype(
        jnp.bfloat16
    )


def body(x_tiles, tile_pos, valid_rows, stem_w, dw_kernel, norm_gain, w_in, w_out, cotangent):
    f32 = jnp.float32
    bf16 = jnp.bfloat16
    lat_count = lax.axis_size("lat")
    per_pair = (K_TILES + lat_count - 1) // lat_count
    slot_count = lat_count * per_pair
    cells = TS * TS
    inputs = x_tiles[0]
    places = tile_pos[0]
    ocean_rows = valid_rows[0]
    upstream = cotangent[0]
    tile_count = inputs.shape[0]
    cell_rows = jnp.arange(cells, dtype=jnp.int32) // TS
    ocean = cell_rows[None, :] < ocean_rows[:, None]
    masked_in = jnp.where(ocean[:, None, :], inputs, jnp.zeros_like(inputs))
    stem_tiles = jnp.einsum("kc,akp->acp", stem_w, masked_in, preferred_element_type=f32).astype(
        bf16
    )
    band_of = places // K_TILES
    local_place = places - band_of * K_TILES
    tile_order = jnp.arange(tile_count, dtype=jnp.int32)
    earlier = (band_of[None, :] == band_of[:, None]) & (tile_order[None, :] < tile_order[:, None])
    rank_in = jnp.sum(earlier.astype(jnp.int32), axis=1)
    slot_of = band_of * per_pair + rank_in
    route_map = jnp.arange(slot_count, dtype=jnp.int32)[:, None] == slot_of[None, :]
    route_b = route_map.astype(bf16)
    slot_place = jnp.sum(jnp.where(route_map, local_place[None, :] + 1, 0), axis=1) - 1
    slot_place = slot_place.reshape(lat_count, per_pair)
    outgoing = select_rows(route_b, masked_in).reshape(lat_count, per_pair, CIN, cells)
    arrived_raw, arrived_place = (
        lax.all_to_all(outgoing, "lat", split_axis=0, concat_axis=0, tiled=True),
        lax.all_to_all(slot_place, "lat", split_axis=0, concat_axis=0, tiled=True),
    )
    arrived_raw = arrived_raw.reshape(slot_count, CIN, cells)
    arrived = jnp.einsum("kc,akp->acp", stem_w, arrived_raw, preferred_element_type=f32).astype(
        bf16
    )
    placing = (
        jnp.arange(K_TILES, dtype=jnp.int32)[:, None] == arrived_place.reshape(slot_count)[None, :]
    )
    placing_b = placing.astype(bf16)
    band_field = tiles_to_block(select_rows(placing_b, arrived))
    reach = KW // 2
    widened = extended(band_field, (("lon", 2),), reach, True)
    padded = extended(widened, (("lat", 1),), reach, False)

    def window(tap_index):
        row_off = tap_index // KW
        col_off = tap_index % KW
        return padded[:, row_off : row_off + BH, col_off : col_off + BW].astype(f32)

    conv_out = jnp.zeros(band_field.shape, f32)
    for tap_index in range(KW * KW):
        conv_out = conv_out + dw_kernel[:, tap_index][:, None, None] * window(tap_index)
    centred = conv_out - jnp.mean(conv_out, axis=0, keepdims=True)
    inv_std = lax.rsqrt(jnp.mean(centred * centred, axis=0, keepdims=True) + 1e-06)
    unit = centred * inv_std
    normed = (unit * norm_gain[:, None, None]).astype(bf16)
    returning = select_rows(placing_b.T, block_to_tiles(normed)).reshape(
        lat_count, per_pair, C, cells
    )
    returned = lax.all_to_all(returning, "lat", split_axis=0, concat_axis=0, tiled=True).reshape(
        slot_count, C, cells
    )
    features = select_rows(route_b.T, returned)
    preact = jnp.einsum("ch,acp->ahp", w_in, features, preferred_element_type=f32)
    hidden = gelu_tanh(preact).astype(bf16)
    branch = jnp.einsum("hc,ahp->acp", w_out, hidden, preferred_element_type=f32)
    result = jnp.where(ocean[:, None, :], stem_tiles.astype(f32) + branch, 0.0).astype(bf16)
    masked_grad = jnp.where(ocean[:, None, :], upstream, jnp.zeros_like(upstream))
    grad_hidden = jnp.einsum("hc,acp->ahp", w_out, masked_grad, preferred_element_type=f32)
    grad_preact = jax.vjp(gelu_tanh, preact)[1](grad_hidden)[0].astype(bf16)
    grad_feats = jnp.einsum("ch,ahp->acp", w_in, grad_preact, preferred_element_type=f32).astype(
        bf16
    )
    grad_outgoing = select_rows(route_b, grad_feats).reshape(lat_count, per_pair, C, cells)
    grad_arrived = lax.all_to_all(
        grad_outgoing, "lat", split_axis=0, concat_axis=0, tiled=True
    ).reshape(slot_count, C, cells)
    sum_in = jnp.einsum("acp,ahp->ch", features, grad_preact, preferred_element_type=f32)
    sum_out = jnp.einsum("ahp,acp->hc", hidden, masked_grad, preferred_element_type=f32)
    grad_field = tiles_to_block(select_rows(placing_b, grad_arrived)).astype(f32)
    scaled = grad_field * norm_gain[:, None, None]
    grad_conv = inv_std * (
        scaled
        - jnp.mean(scaled, axis=0, keepdims=True)
        - unit * jnp.mean(scaled * unit, axis=0, keepdims=True)
    )
    kernel_terms = []
    for tap_index in range(KW * KW):
        kernel_terms.append(jnp.sum(grad_conv * window(tap_index), axis=(1, 2)))
    sum_kernel = jnp.stack(kernel_terms, axis=1)
    sum_gain = jnp.sum(grad_field * unit, axis=(1, 2))
    cell_sum = TS * jnp.sum(ocean_rows.astype(f32))
    total_in, total_out, total_kernel, total_gain, cell_total = lax.psum(
        (sum_in, sum_out, sum_kernel, sum_gain, cell_sum), ("lat", "lon")
    )
    return (
        result[None],
        total_in / cell_total,
        total_out / cell_total,
        total_kernel / cell_total,
        total_gain / cell_total,
    )


def solution(mesh):
    in_specs = (
        P("lon", "lat", None, None),
        P("lon", "lat"),
        P("lon", "lat"),
        P(),
        P(),
        P(),
        P(),
        P(),
        P("lon", "lat", None, None),
    )
    out_specs = (P("lon", "lat", None, None), P(), P(), P(), P())
    return jax.shard_map(body, mesh=mesh, in_specs=in_specs, out_specs=out_specs, check_vma=False)
```

profile of v0, /device:TPU:2, one launch (start us, length us, event | category | flops | bytes accessed | tf_op | source)
XLA Modules:
  0.0 583.2 jit_solution(11858804636175604378)
XLA Ops:
  7.2 0.7 and_select_fusion
  7.9 0.7 add_bitcast_fusion
  8.9 0.7 sub.49
  9.6 6.2 %all-to-all-start = ((s32[16,1,2]{2,1,0:T(1,128)}), s32[16,1,2]{2,1,0:T(1,128)S(1)}, u32[]{:S(2)}, u32[]{:S(2)}) async-start(s32[16,1,2]{2,1,0:T(1,128)} %bitcast.9), calls=%async_computation | async-start | bytes 16384 | tf_op jit(solution)/shard_map/all_to_all | solution.py:83
  15.8 0.7 broadcast_compare_fusion
  16.5 1.0 bitcast_select_fusion.3
  17.5 0.6 convolution_convert_fusion.2
  18.6 1.9 copy.69
  20.5 5.7 all-to-all-start.1
  26.8 0.7 reduce.5
  27.6 15.3 %all-to-all-done.1 = bf16[16,2,77,256]{3,1,2,0:T(2,128)(2,1)S(1)} async-done(((bf16[16,2,77,256]{3,1,2,0:T(2,128)(2,1)}), bf16[16,2,77,256]{3,1,2,0:T(2,128)(2,1)S(1)}, u32[]{:S(2)}, u32[]{:S(2)}) %all-to-all-start.1) | async-done | bytes 1261600 | tf_op jit(solution)/shard_map/all_to_all | solution.py:82
  43.1 1.1 convert_bitcast_fusion
  44.2 2.7 fusion.114
  46.9 7.2 %copy.72 = bf16[32,200,256]{1,2,0:T(8,128)(2,1)} copy(bf16[32,200,256]{2,0,1:T(8,128)(2,1)} %fusion.114) | data formatting | bytes 6553600 | tf_op jit(solution)/shard_map/convert_element_type | solution.py:47
  54.1 2.8 copy.73
  57.0 1.6 collective-permute-start
  58.7 4.5 collective-permute-start.1
  63.3 3.1 collective-permute-done
  66.5 1.9 collective-permute-start.2
  68.4 4.7 collective-permute-start.3
  73.1 1.4 collective-permute-done.2
  74.5 1.7 collective-permute-done.3
  76.2 8.1 %maximum_maximum_fusion = (bf16[200,67,134]{0,2,1:T(8,128)(2,1)S(1)}, bf16[200,67,134]{0,2,1:T(8,128)(2,1)S(1)}) fusion(bf16[200,64,3]{0,2,1:T(4,128)(2,1)S(1)} %collective-permute-done.1, bf16[200,64,128]{0,2,1:T(8,128)(2,1)S(1)} %bitcast.228, bf16[200,64,3]{0,2,1:T(4,128)(2,1)S(1)} %collective-permute-done, ...), kind=kLoop, calls=%fused_computation.208 | loop fusion | flops 28729600 | bytes 10934400 | tf_op jit(solution)/shard_map/concatenate | solution.py:26
  84.3 68.1 %fusion.152 = (f32[64,128]{1,0:T(8,128)S(1)}, f32[200,64,128]{0,2,1:T(8,128)S(1)}) fusion(bf16[200,67,134]{0,2,1:T(8,128)(2,1)S(1)} %get-tuple-element.77, f32[200]{0:T(256)S(1)} %bitcast.286, f32[200]{0:T(256)S(1)} %bitcast.287, f32[200]{0:T(256)S(1)} %bitcast.240, f32[200]{0:T(256)S(1)} %bitcast.241, f32[200]{0:T(256)S(1)} %bitcast.242, ...), kind=kLoop, calls=%fused_computation.307 | loop fusion | flops 270327808 | bytes 147681568 | tf_op jit(solution)/shard_map/reduce_sum | solution.py:106
  152.5 2.5 multiply_reduce_fusion.3
  155.0 2.6 multiply_convert_fusion
  157.6 2.6 copy.74
  160.2 7.3 %copy.76 = bf16[32,200,256]{2,0,1:T(8,128)(2,1)} copy(bf16[32,200,256]{1,2,0:T(8,128)(2,1)} %bitcast.237) | data formatting | bytes 6553600 | tf_op jit(solution)/shard_map/reshape | solution.py:43
  167.4 4.8 convolution_convert_fusion.1
  172.2 7.5 %reshape.217 = bf16[16,2,200,256]{3,1,0,2:T(2,128)(2,1)} reshape(bf16[32,200,256]{2,0,1:T(8,128)(2,1)} %convolution_convert_fusion.1) | data formatting | bytes 6553600 | tf_op jit(solution)/shard_map/reshape | solution.py:110
  179.8 4.2 copy.77
  183.9 45.5 %all_to_all.21 = bf16[16,2,200,256]{3,1,2,0:T(2,128)(2,1)S(1)} all-to-all(bf16[16,2,200,256]{3,1,2,0:T(2,128)(2,1)S(1)} %copy.77), channel_id=1, replica_groups=mesh['lat'=16,'lon'=8] {'lat'}, dimensions={0} | all-to-all | bytes 6553600 | tf_op jit(solution)/shard_map/all_to_all | solution.py:113
  229.4 5.5 copy.78
  234.9 7.8 %reshape.218 = bf16[32,200,256]{2,0,1:T(8,128)(2,1)} reshape(bf16[16,2,200,256]{3,1,0,2:T(2,128)(2,1)} %copy.78) | data formatting | bytes 6553600 | tf_op jit(solution)/shard_map/reshape | solution.py:113
  242.8 2.5 convolution_convert_fusion.4
  245.3 0.6 fusion.124
  246.0 3.7 fusion.107
  249.7 0.6 fusion.120
  250.3 2.8 convolution_convert_fusion
  253.1 7.6 %reshape.219 = bf16[16,2,200,256]{3,1,0,2:T(2,128)(2,1)} reshape(bf16[32,200,256]{2,0,1:T(8,128)(2,1)} %convolution_convert_fusion) | data formatting | bytes 6553600 | tf_op jit(solution)/shard_map/reshape | solution.py:127
  260.7 5.8 %copy.82 = bf16[16,2,200,256]{3,1,2,0:T(2,128)(2,1)} copy(bf16[16,2,200,256]{3,1,0,2:T(2,128)(2,1)} %reshape.219) | data formatting | bytes 6553600 | tf_op jit(solution)/shard_map/reshape | solution.py:127
  266.5 6.0 %all-to-all-start.3 = ((bf16[16,2,200,256]{3,1,2,0:T(2,128)(2,1)}), bf16[16,2,200,256]{3,1,2,0:T(2,128)(2,1)}, u32[]{:S(2)}, u32[]{:S(2)}) async-start(bf16[16,2,200,256]{3,1,2,0:T(2,128)(2,1)} %copy.82), calls=%async_computation.3 | async-start | bytes 6553600 | tf_op jit(solution)/shard_map/all_to_all | solution.py:128
  272.6 0.6 convert_reduce_fusion.1
  273.8 1.2 fusion.119
  275.1 1.6 convolution_bitcast_fusion.1
  276.7 4.2 convolution_bitcast_fusion
  280.9 4.0 fusion.121
  285.0 27.7 %all-to-all-done.3 = bf16[16,2,200,256]{3,1,2,0:T(2,128)(2,1)} async-done(((bf16[16,2,200,256]{3,1,2,0:T(2,128)(2,1)}), bf16[16,2,200,256]{3,1,2,0:T(2,128)(2,1)}, u32[]{:S(2)}, u32[]{:S(2)}) %all-to-all-start.3) | async-done | bytes 3276832 | tf_op jit(solution)/shard_map/all_to_all | solution.py:128
  312.7 7.5 %copy.83 = bf16[16,2,200,256]{3,1,0,2:T(2,128)(2,1)} copy(bf16[16,2,200,256]{3,1,2,0:T(2,128)(2,1)} %all-to-all-done.3) | data formatting | bytes 6553600 | tf_op jit(solution)/shard_map/all_to_all | solution.py:128
  320.1 7.8 %reshape.220 = bf16[32,200,256]{2,0,1:T(8,128)(2,1)} reshape(bf16[16,2,200,256]{3,1,0,2:T(2,128)(2,1)} %copy.83) | data formatting | bytes 6553600 | tf_op jit(solution)/shard_map/reshape | solution.py:130
  327.9 5.7 convert_convert_fusion
  333.6 9.3 %copy.84 = f32[32,200,256]{1,2,0:T(8,128)} copy(f32[32,200,256]{2,0,1:T(8,128)} %convert_convert_fusion) | data formatting | bytes 13107200 | tf_op jit(solution)/shard_map/convert_element_type | solution.py:133
  342.9 4.6 multiply_reduce_fusion.2
  347.7 4.4 copy.85
  352.1 8.8 %multiply_reduce_fusion = (f32[200]{0:T(256)S(1)}, f32[64,128]{1,0:T(8,128)S(1)}) fusion(f32[200,64,128]{0,2,1:T(8,128)S(1)} %bitcast.231, f32[200,64,128]{0,2,1:T(8,128)} %copy-done.4, f32[64,128]{1,0:T(8,128)S(1)} %add_rsqrt_fusion, f32[64,128]{1,0:T(8,128)S(1)} %broadcast_multiply_fusion.1, f32[200]{0:T(256)S(1)} %copy-done.12), kind=kLoop, calls=%fused_computation.195 | loop fusion | flops 11460408 | bytes 13207104 | tf_op jit(solution)/shard_map/reduce_sum | solution.py:144
  360.9 50.6 %fusion.96 = (f32[200]{0:T(256)S(1)}, f32[200]{0:T(256)S(1)}, f32[200]{0:T(256)S(1)}, f32[200]{0:T(256)S(1)}, f32[200]{0:T(256)S(1)}, /*index=5*/f32[200]{0:T(25...) fusion(bf16[200,67,134]{0,2,1:T(8,128)(2,1)} %copy-done.3, ...), kind=kLoop, calls=%fused_computation.194 | loop fusion | flops 99938800 | bytes 78789472 | tf_op jit(solution)/shard_map/reduce_sum | solution.py:142
  411.5 49.7 %fusion.45 = (f32[200]{0:T(256)S(1)}, f32[200]{0:T(256)S(1)}, f32[200]{0:T(256)S(1)}, f32[200]{0:T(256)S(1)}, f32[200]{0:T(256)S(1)}, /*index=5*/f32[200]{0:T(25...) fusion(f32[200,64,128]{0,2,1:T(8,128)} %get-tuple-element.71, ...), kind=kLoop, calls=%fused_computation.143 | loop fusion | flops 88470000 | bytes 65550400 | tf_op jit(solution)/shard_map/reduce_sum | solution.py:142
  461.3 27.5 %fusion.78 = (f32[200]{0:T(256)S(1)}, f32[200]{0:T(256)S(1)}, f32[200]{0:T(256)S(1)}, f32[200]{0:T(256)S(1)}, f32[200]{0:T(256)S(1)}, /*index=5*/f32[200]{0:T(25...) fusion(f32[200,64,128]{0,2,1:T(8,128)} %get-tuple-element.71, ...), kind=kLoop, calls=%fused_computation.176 | loop fusion | flops 78641200 | bytes 19822400 | tf_op jit(solution)/shard_map/reduce_sum | solution.py:142
  488.9 4.3 fusion.27
  493.4 74.8 %all-reduce = (f32[]{:T(128)}, f32[200,49]{0,1:T(8,128)S(1)}, f32[200]{0:T(256)S(1)}) all-reduce(f32[]{:T(128)S(6)} %mul_shard_map.3, f32[200,49]{0,1:T(8,128)S(1)} %stack.199, f32[200]{0:T(256)S(1)} %get-tuple-element.5), channel_id=1, replica_groups=mesh['lat'=16,'lon'=8] {'lat','lon'}, use_global_device_ids=true, to_apply=%region_6.7 | all-reduce | flops 10001 | bytes 80008 | tf_op jit(solution)/shard_map/psum | solution.py:146
  568.2 2.7 broadcast_divide_fusion
  570.9 2.7 broadcast_divide_fusion.1
  573.6 1.3 broadcast_divide_fusion.2
  574.9 1.3 broadcast_divide_fusion.3
  (61 shorter events, 2.5 us)
Async XLA Ops:
  7.2 238.1 %copy-start = (bf16[200,800]{1,0:T(8,128)(2,1)S(1)}, bf16[200,800]{1,0:T(8,128)(2,1)}, u32[]{:S(2)}) copy-start(bf16[200,800]{1,0:T(8,128)(2,1)} %param.15) | copy-start | bytes 960004
  7.2 19.1 %copy-start.11 = (f32[200,49]{0,1:T(8,128)S(1)}, f32[200,49]{0,1:T(8,128)}, u32[]{:S(2)}) copy-start(f32[200,49]{0,1:T(8,128)} %param.13) | copy-start | bytes 117604
  7.2 35.9 %copy-start.10 = (bf16[77,200]{1,0:T(8,128)(2,1)S(1)}, bf16[77,200]{1,0:T(8,128)(2,1)}, u32[]{:S(2)}) copy-start(bf16[77,200]{1,0:T(8,128)(2,1)} %param.12) | copy-start | bytes 92404
  9.6 11.0 %all-to-all-start = ((s32[16,1,2]{2,1,0:T(1,128)}), s32[16,1,2]{2,1,0:T(1,128)S(1)}, u32[]{:S(2)}, u32[]{:S(2)}) async-start(s32[16,1,2]{2,1,0:T(1,128)} %bitcast.9), calls=%async_computation | async-start | bytes 16384 | tf_op jit(solution)/shard_map/all_to_all | solution.py:83
  20.5 22.4 %all-to-all-start.1 = ((bf16[16,2,77,256]{3,1,2,0:T(2,128)(2,1)}), bf16[16,2,77,256]{3,1,2,0:T(2,128)(2,1)S(1)}, u32[]{:S(2)}, u32[]{:S(2)}) async-start(bf16[16,2,77,256]{3,1,2,0:T(2,128)(2,1)} %copy.69), calls=%async_computation.1 | async-start | bytes 2523136 | tf_op jit(solution)/shard_map/all_to_all | solution.py:82
  56.9 27.4 %copy-start.6 = (bf16[200,4,16,8,16]{0,4,3,2,1:T(8,128)(2,1)}, bf16[200,4,16,8,16]{0,4,3,2,1:T(8,128)(2,1)S(1)}, u32[]{:S(2)}) copy-start(bf16[200,4,16,8,16]{0,4,3,2,1:T(8,128)(2,1)S(1)} %copy.73) | copy-start | bytes 9830404
  57.0 9.3 %collective-permute-start = (bf16[200,64,3]{0,2,1:T(4,128)(2,1)S(1)}, bf16[200,64,3]{0,2,1:T(4,128)(2,1)S(1)}, u32[]{:S(2)}, u32[]{:S(2)}) collective-permute-start(bf16[200,64,3]{0,2,1:T(4,128)(2,1)S(1)} %get-tuple-element.80), channel_id=1, source_target_pairs={{0,1},{1,2},{2,3},{3,4},{4,5},{5,6},{6,7},{7,0},{8,9},{9,10},{10,1... | collective-permute-start | bytes 230408 | tf_op jit(solution)/shard_map/ppermute | solution.py:22
  58.7 7.6 %collective-permute-start.1 = (bf16[200,64,3]{0,2,1:T(4,128)(2,1)S(1)}, bf16[200,64,3]{0,2,1:T(4,128)(2,1)S(1)}, u32[]{:S(2)}, u32[]{:S(2)}) collective-permute-start(bf16[200,64,3]{0,2,1:T(4,128)(2,1)S(1)} %get-tuple-element.81), channel_id=1, source_target_pairs={{1,0},{2,1},{3,2},{4,3},{5,4},{6,5},{7,6},{0,7},{9,8},{10,9},{11,1... | collective-permute-start | bytes 230408 | tf_op jit(solution)/shard_map/ppermute | solution.py:25
  66.5 8.0 %collective-permute-start.2 = (bf16[200,3,134]{0,2,1:T(8,128)(2,1)S(1)}, bf16[200,3,134]{0,2,1:T(8,128)(2,1)S(1)}, u32[]{:S(2)}, u32[]{:S(2)}) collective-permute-start(bf16[200,3,134]{0,2,1:T(8,128)(2,1)S(1)} %get-tuple-element.78), channel_id=1, source_target_pairs={{0,8},{8,16},{16,24},{24,32},{32,40},{40,48},{48,56},{56,64},{64,7... | collective-permute-start | bytes 482408 | tf_op jit(solution)/shard_map/ppermute | solution.py:22
  68.4 7.8 %collective-permute-start.3 = (bf16[200,3,134]{0,2,1:T(8,128)(2,1)S(1)}, bf16[200,3,134]{0,2,1:T(8,128)(2,1)S(1)}, u32[]{:S(2)}, u32[]{:S(2)}) collective-permute-start(bf16[200,3,134]{0,2,1:T(8,128)(2,1)S(1)} %get-tuple-element.79), channel_id=1, source_target_pairs={{8,0},{16,8},{24,16},{32,24},{40,32},{48,40},{56,48},{64,56},{72,6... | collective-permute-start | bytes 482408 | tf_op jit(solution)/shard_map/ppermute | solution.py:25
  84.3 68.1 %copy-start.2 = (bf16[200,67,134]{0,2,1:T(8,128)(2,1)}, bf16[200,67,134]{0,2,1:T(8,128)(2,1)S(1)}, u32[]{:S(2)}) copy-start(bf16[200,67,134]{0,2,1:T(8,128)(2,1)S(1)} %get-tuple-element.76) | copy-start | bytes 10773604
  84.3 68.1 %copy-start.3 = (bf16[200,67,134]{0,2,1:T(8,128)(2,1)}, bf16[200,67,134]{0,2,1:T(8,128)(2,1)S(1)}, u32[]{:S(2)}) copy-start(bf16[200,67,134]{0,2,1:T(8,128)(2,1)S(1)} %get-tuple-element.77) | copy-start | bytes 10773604
  152.5 5.1 copy-start.4
  152.5 2.5 copy-start.12
  234.9 11.0 %copy-start.14 = (bf16[800,200]{0,1:T(8,128)(2,1)S(1)}, bf16[800,200]{0,1:T(8,128)(2,1)}, u32[]{:S(2)}) copy-start(bf16[800,200]{0,1:T(8,128)(2,1)} %param.16) | copy-start | bytes 960004
  246.0 3.7 copy-start.8
  253.1 19.4 %copy-start.13 = (s32[1,4]{1,0:T(1,128)S(1)}, s32[1,4]{1,0:T(1,128)}, u32[]{:S(2)}) copy-start(s32[1,4]{1,0:T(1,128)} %param.11) | copy-start | bytes 52
  266.5 46.1 %all-to-all-start.3 = ((bf16[16,2,200,256]{3,1,2,0:T(2,128)(2,1)}), bf16[16,2,200,256]{3,1,2,0:T(2,128)(2,1)}, u32[]{:S(2)}, u32[]{:S(2)}) async-start(bf16[16,2,200,256]{3,1,2,0:T(2,128)(2,1)} %copy.82), calls=%async_computation.3 | async-start | bytes 6553600 | tf_op jit(solution)/shard_map/all_to_all | solution.py:128
  272.5 295.6 %all-reduce.4.cloned.1.call-start = ((), (), s32[]{:S(2)}) async-start(), calls=%async_computation.4 | async-start | bytes 2867200 | tf_op jit(solution)/shard_map/psum | solution.py:146
  276.7 4.3 copy-start.9
  352.1 8.8 %copy-start.7 = (f32[200,4,16,8,16]{0,4,3,2,1:T(8,128)}, f32[200,4,16,8,16]{0,4,3,2,1:T(8,128)S(1)}, u32[]{:S(2)}) copy-start(f32[200,4,16,8,16]{0,4,3,2,1:T(8,128)S(1)} %copy.85) | copy-start | bytes 19660804
  360.9 127.9 %slice-start = ((s8[4665344]{0:T(1024)(128)(4,1)}), s8[471040]{0:T(1024)(128)(4,1)S(1)}, s32[]{:S(2)}) async-start(s8[4665344]{0:T(1024)(128)(4,1)} %bitcast.224), calls=%async_computation.5 | async-start | bytes 942080
  411.5 77.3 %slice-start.1 = ((s8[4665344]{0:T(1024)(128)(4,1)}), s8[4194304]{0:T(1024)(128)(4,1)S(1)}, s32[]{:S(2)}) async-start(s8[4665344]{0:T(1024)(128)(4,1)} %bitcast.224), calls=%async_computation.6 | async-start | bytes 8388608
  461.3 27.6 %copy-start.5 = (f32[200,64,128]{0,2,1:T(8,128)S(1)}, f32[200,64,128]{0,2,1:T(8,128)}, u32[]{:S(2)}) copy-start(f32[200,64,128]{0,2,1:T(8,128)} %get-tuple-element.71) | copy-start | bytes 19660804
  461.3 114.9 %copy-start.1 = (bf16[200,800]{1,0:T(8,128)(2,1)S(1)}, bf16[200,800]{1,0:T(8,128)(2,1)}, u32[]{:S(2)}) copy-start(bf16[200,800]{1,0:T(8,128)(2,1)} %param.15) | copy-start | bytes 960004
Sparse Core Ops, SparseCore 0:
  281.1 168.1 all-reduce.3
where the time goes:
time: 590 us; the launch traced here: 583 us
  other arithmetic  240 us (41%)
  blocking collectives  120 us (20%)
  local copies, waits for them, and re-layouts  91.8 us (16%)
  waiting for transfers between devices  49.2 us (8%)
  matrix products  36.2 us (6%)
  starting transfers between devices  30.8 us (5%)
  between operations  15.4 us (3%)
    reduce_sum x4, other arithmetic, body(): kernel_terms.append(jnp.sum(grad_conv * window(tap_index), axis=(1, 2)))  132 us
    psum x1, blocking collectives, body(): lax.psum((sum_in, sum_out, sum_kernel, sum_gain, cell_sum), ('lat', 'lon'))  74.8 us
    reduce_sum x1, other arithmetic, body(): centred = conv_out - jnp.mean(conv_out, axis=0, keepdims=True)  68.1 us
    all_to_all x1, blocking collectives, body(): lax.all_to_all(returning, 'lat', split_axis=0, concat_axis=0, tiled=True)  45.5 us
    all_to_all x1, waiting for transfers between devices, body(): lax.all_to_all(grad_outgoing, 'lat', split_axis=0, concat_axis=0, tiled=T...  27.7 us
    dot_general x6, matrix products, select_rows(): jnp.einsum('qa,acp->qcp', onehot, tiles, preferred_element_type=jnp.float32)  19.1 us
    all_to_all x1, waiting for transfers between devices, body(): lax.all_to_all(outgoing, 'lat', split_axis=0, concat_axis=0, tiled=True)  15.3 us
    convert_element_type x2, local copies, waits for them, and re-layouts, body(): tiles_to_block(select_rows(placing_b, grad_arrived)).astype(f32)  13.7 us
  transfers between devices with their start and end apart: 8, of which 5 were waited for; matrix products, arithmetic and copies ran while one was open for 34% of the time, Pallas kernels for 0%

commit v1 on v0

--- a/solution.py
+++ b/solution.py
@@ -2,6 +2,7 @@
 import jax.numpy as jnp
 from jax import lax
 from jax.sharding import PartitionSpec as P
+from jax.lax import psum
 
 C = 200
 CIN = 77
@@ -143,8 +144,13 @@
     sum_kernel = jnp.stack(kernel_terms, axis=1)
     sum_gain = jnp.sum(grad_field * unit, axis=(1, 2))
     cell_sum = TS * jnp.sum(ocean_rows.astype(f32))
-    total_in, total_out, total_kernel, total_gain, cell_total = lax.psum(
-        (sum_in, sum_out, sum_kernel, sum_gain, cell_sum), ("lat", "lon")
+
+    def _touch_entries(view):
+        block_now = psum(psum(view, axis_name="lon"), axis_name="lat")
+        return block_now
+
+    total_in, total_out, total_kernel, total_gain, cell_total = _touch_entries(
+        (sum_in, sum_out, sum_kernel, sum_gain, cell_sum)
     )
     return (
         result[None],

time: 590 us -> 674 us (1.14)
  the two profiles are of different devices: /device:TPU:2 before, /device:TPU:0 now
where the time goes in v1:
time: 674 us; the launch traced here: 667 us
  other arithmetic  240 us (36%)
  blocking collectives  141 us (21%)
  waiting for transfers between devices  120 us (18%)
  local copies, waits for them, and re-layouts  91.8 us (14%)
  matrix products  35.3 us (5%)
  starting transfers between devices  24.1 us (4%)
  between operations  15.5 us (2%)
    reduce_sum x4, other arithmetic, body(): kernel_terms.append(jnp.sum(grad_conv * window(tap_index), axis=(1, 2)))  132 us
    psum x2, waiting for transfers between devices, _touch_entries(): block_now = psum(psum(view, axis_name='lon'), axis_name='lat')  95.2 us
    psum x2, blocking collectives, _touch_entries(): block_now = psum(psum(view, axis_name='lon'), axis_name='lat')  92 us
    reduce_sum x1, other arithmetic, body(): centred = conv_out - jnp.mean(conv_out, axis=0, keepdims=True)  68.1 us
    all_to_all x1, blocking collectives, body(): lax.all_to_all(returning, 'lat', split_axis=0, concat_axis=0, tiled=True)  48.9 us
    dot_general x6, matrix products, select_rows(): jnp.einsum('qa,acp->qcp', onehot, tiles, preferred_element_type=jnp.float32)  19.1 us
    all_to_all x1, waiting for transfers between devices, body(): lax.all_to_all(outgoing, 'lat', split_axis=0, concat_axis=0, tiled=True)  17.4 us
    convert_element_type x2, local copies, waits for them, and re-layouts, body(): tiles_to_block(select_rows(placing_b, grad_arrived)).astype(f32)  13.8 us
  transfers between devices with their start and end apart: 9, of which 5 were waited for; matrix products, arithmetic and copies ran while one was open for 30% of the time, Pallas kernels for 0%

profile of v1, /device:TPU:0, one launch (start us, length us, event | category | flops | bytes accessed | tf_op | source)
XLA Modules:
  0.0 666.9 jit_solution(17828282939719616431)
XLA Ops:
  7.2 0.7 and_select_fusion
  7.9 0.7 add_bitcast_fusion
  8.9 0.7 sub.49
  9.6 5.9 all-to-all-start
  15.4 0.7 broadcast_compare_fusion
  16.2 1.0 bitcast_select_fusion.3
  17.2 0.6 convolution_convert_fusion.2
  18.3 1.9 copy.69
  20.2 1.2 all-to-all-done
  21.4 4.5 all-to-all-start.1
  26.5 0.7 reduce.5
  27.3 17.4 %all-to-all-done.1 = bf16[16,2,77,256]{3,1,2,0:T(2,128)(2,1)S(1)} async-done(((bf16[16,2,77,256]{3,1,2,0:T(2,128)(2,1)}), bf16[16,2,77,256]{3,1,2,0:T(2,128)(2,1)S(1)}, u32[]{:S(2)}, u32[]{:S(2)}) %all-to-all-start.1) | async-done | bytes 1261600 | tf_op jit(solution)/shard_map/all_to_all | solution.py:83
  44.9 1.1 convert_bitcast_fusion
  46.0 2.7 fusion.114
  48.7 7.2 %copy.72 = bf16[32,200,256]{1,2,0:T(8,128)(2,1)} copy(bf16[32,200,256]{2,0,1:T(8,128)(2,1)} %fusion.114) | data formatting | bytes 6553600 | tf_op jit(solution)/shard_map/convert_element_type | solution.py:48
  55.9 2.8 copy.73
  58.8 1.6 collective-permute-start
  60.5 4.5 collective-permute-start.1
  65.0 3.1 collective-permute-done
  68.2 1.3 collective-permute-start.2
  69.5 1.5 collective-permute-start.3
  71.1 2.9 collective-permute-done.3
  73.9 8.1 %maximum_maximum_fusion = (bf16[200,67,134]{0,2,1:T(8,128)(2,1)S(1)}, bf16[200,67,134]{0,2,1:T(8,128)(2,1)S(1)}) fusion(bf16[200,64,3]{0,2,1:T(4,128)(2,1)S(1)} %collective-permute-done.1, bf16[200,64,128]{0,2,1:T(8,128)(2,1)S(1)} %bitcast.228, bf16[200,64,3]{0,2,1:T(4,128)(2,1)S(1)} %collective-permute-done, ...), kind=kLoop, calls=%fused_computation.208 | loop fusion | flops 28729600 | bytes 10934400 | tf_op jit(solution)/shard_map/concatenate | solution.py:27
  82.0 68.1 %fusion.152 = (f32[64,128]{1,0:T(8,128)S(1)}, f32[200,64,128]{0,2,1:T(8,128)S(1)}) fusion(bf16[200,67,134]{0,2,1:T(8,128)(2,1)S(1)} %get-tuple-element.82, f32[200]{0:T(256)S(1)} %bitcast.286, f32[200]{0:T(256)S(1)} %bitcast.287, f32[200]{0:T(256)S(1)} %bitcast.240, f32[200]{0:T(256)S(1)} %bitcast.241, f32[200]{0:T(256)S(1)} %bitcast.242, ...), kind=kLoop, calls=%fused_computation.307 | loop fusion | flops 270327808 | bytes 147681568 | tf_op jit(solution)/shard_map/reduce_sum | solution.py:107
  150.2 2.5 multiply_reduce_fusion.3
  152.7 2.6 multiply_convert_fusion
  155.3 2.6 copy.74
  157.9 7.3 %copy.76 = bf16[32,200,256]{2,0,1:T(8,128)(2,1)} copy(bf16[32,200,256]{1,2,0:T(8,128)(2,1)} %bitcast.237) | data formatting | bytes 6553600 | tf_op jit(solution)/shard_map/reshape | solution.py:44
  165.1 4.8 convolution_convert_fusion.1
  169.9 7.5 %reshape.217 = bf16[16,2,200,256]{3,1,0,2:T(2,128)(2,1)} reshape(bf16[32,200,256]{2,0,1:T(8,128)(2,1)} %convolution_convert_fusion.1) | data formatting | bytes 6553600 | tf_op jit(solution)/shard_map/reshape | solution.py:111
  177.5 4.2 copy.77
  181.6 48.9 %all_to_all.21 = bf16[16,2,200,256]{3,1,2,0:T(2,128)(2,1)S(1)} all-to-all(bf16[16,2,200,256]{3,1,2,0:T(2,128)(2,1)S(1)} %copy.77), channel_id=1, replica_groups=mesh['lat'=16,'lon'=8] {'lat'}, dimensions={0} | all-to-all | bytes 6553600 | tf_op jit(solution)/shard_map/all_to_all | solution.py:114
  230.6 5.5 copy.78
  236.1 7.8 %reshape.218 = bf16[32,200,256]{2,0,1:T(8,128)(2,1)} reshape(bf16[16,2,200,256]{3,1,0,2:T(2,128)(2,1)} %copy.78) | data formatting | bytes 6553600 | tf_op jit(solution)/shard_map/reshape | solution.py:114
  243.9 2.5 convolution_convert_fusion.4
  246.5 0.6 fusion.124
  247.1 3.7 fusion.107
  250.9 0.6 fusion.120
  251.5 2.8 convolution_convert_fusion
  254.3 7.5 %reshape.219 = bf16[16,2,200,256]{3,1,0,2:T(2,128)(2,1)} reshape(bf16[32,200,256]{2,0,1:T(8,128)(2,1)} %convolution_convert_fusion) | data formatting | bytes 6553600 | tf_op jit(solution)/shard_map/reshape | solution.py:128
  261.8 5.8 copy.82
  267.7 4.7 all-to-all-start.3
  272.4 1.6 convolution_bitcast_fusion.1
  274.0 4.2 convolution_bitcast_fusion
  278.3 0.6 convert_reduce_fusion.1
  279.8 4.0 fusion.121
  283.9 95.2 %all-reduce.9.cloned.1.call-done = (f32[200,800]{1,0:T(8,128)}, f32[800,200]{0,1:T(8,128)}) async-done(((f32[200,800]{1,0:T(8,128)}, f32[800,200]{0,1:T(8,128)}), (f32[200,800]{1,0:T(8,128)}, f32[800,200]{0,1:T(8,128)})) %all-reduce.9.cloned.1.call-update) | async-done | bytes 1280016 | tf_op jit(solution)/shard_map/psum | solution.py:149
  379.1 7.4 %copy.83 = bf16[16,2,200,256]{3,1,0,2:T(2,128)(2,1)} copy(bf16[16,2,200,256]{3,1,2,0:T(2,128)(2,1)} %all-to-all-done.3) | data formatting | bytes 6553600 | tf_op jit(solution)/shard_map/all_to_all | solution.py:129
  386.5 7.8 %reshape.220 = bf16[32,200,256]{2,0,1:T(8,128)(2,1)} reshape(bf16[16,2,200,256]{3,1,0,2:T(2,128)(2,1)} %copy.83) | data formatting | bytes 6553600 | tf_op jit(solution)/shard_map/reshape | solution.py:131
  394.3 5.7 convert_convert_fusion
  400.0 9.3 %copy.84 = f32[32,200,256]{1,2,0:T(8,128)} copy(f32[32,200,256]{2,0,1:T(8,128)} %convert_convert_fusion) | data formatting | bytes 13107200 | tf_op jit(solution)/shard_map/convert_element_type | solution.py:134
  409.3 4.6 multiply_reduce_fusion.2
  414.1 4.4 copy.85
  418.6 8.8 %multiply_reduce_fusion = (f32[200]{0:T(256)S(1)}, f32[64,128]{1,0:T(8,128)S(1)}) fusion(f32[200,64,128]{0,2,1:T(8,128)S(1)} %bitcast.231, f32[200,64,128]{0,2,1:T(8,128)} %copy-done.4, f32[64,128]{1,0:T(8,128)S(1)} %add_rsqrt_fusion, f32[64,128]{1,0:T(8,128)S(1)} %broadcast_multiply_fusion.1, f32[200]{0:T(256)S(1)} %copy-done.11), kind=kLoop, calls=%fused_computation.195 | loop fusion | flops 11460408 | bytes 13207104 | tf_op jit(solution)/shard_map/reduce_sum | solution.py:145
  427.4 50.6 %fusion.96 = (f32[200]{0:T(256)S(1)}, f32[200]{0:T(256)S(1)}, f32[200]{0:T(256)S(1)}, f32[200]{0:T(256)S(1)}, f32[200]{0:T(256)S(1)}, /*index=5*/f32[200]{0:T(25...) fusion(bf16[200,67,134]{0,2,1:T(8,128)(2,1)} %copy-done.3, ...), kind=kLoop, calls=%fused_computation.194 | loop fusion | flops 99938800 | bytes 78789472 | tf_op jit(solution)/shard_map/reduce_sum | solution.py:143
  478.0 49.7 %fusion.45 = (f32[200]{0:T(256)S(1)}, f32[200]{0:T(256)S(1)}, f32[200]{0:T(256)S(1)}, f32[200]{0:T(256)S(1)}, f32[200]{0:T(256)S(1)}, /*index=5*/f32[200]{0:T(25...) fusion(f32[200,64,128]{0,2,1:T(8,128)} %get-tuple-element.76, ...), kind=kLoop, calls=%fused_computation.143 | loop fusion | flops 88470000 | bytes 65550400 | tf_op jit(solution)/shard_map/reduce_sum | solution.py:143
  527.8 27.5 %fusion.78 = (f32[200]{0:T(256)S(1)}, f32[200]{0:T(256)S(1)}, f32[200]{0:T(256)S(1)}, f32[200]{0:T(256)S(1)}, f32[200]{0:T(256)S(1)}, /*index=5*/f32[200]{0:T(25...) fusion(f32[200,64,128]{0,2,1:T(8,128)} %get-tuple-element.76, ...), kind=kLoop, calls=%fused_computation.176 | loop fusion | flops 78641200 | bytes 19822400 | tf_op jit(solution)/shard_map/reduce_sum | solution.py:143
  555.4 4.3 fusion.27
  559.8 39.0 %all-reduce.2 = (f32[]{:T(128)}, f32[200,49]{0,1:T(8,128)S(1)}, f32[200]{0:T(256)S(1)}) all-reduce(f32[]{:T(128)S(6)} %mul_shard_map.3, f32[200,49]{0,1:T(8,128)S(1)} %stack.199, f32[200]{0:T(256)S(1)} %get-tuple-element.5), channel_id=1, replica_groups=mesh['lat'=16,'lon'=8] {'lon'}, use_global_device_ids=true, to_apply=%region_7.8 | all-reduce | flops 10001 | bytes 80008 | tf_op jit(solution)/shard_map/psum | solution.py:149
  598.8 53.0 %all-reduce = (f32[]{:T(128)}, f32[200,49]{0,1:T(8,128)S(1)}, f32[200]{0:T(256)S(1)}) all-reduce(f32[]{:T(128)} %get-tuple-element.71, f32[200,49]{0,1:T(8,128)S(1)} %get-tuple-element.72, f32[200]{0:T(256)S(1)} %get-tuple-element.73), channel_id=1, replica_groups=mesh['lat'=16,'lon'=8] {'lat'}, use_global_device_ids=true, to_apply=%region_8.9 | all-reduce | flops 10001 | bytes 80008 | tf_op jit(solution)/shard_map/psum | solution.py:149
  651.9 2.7 broadcast_divide_fusion
  654.6 2.7 broadcast_divide_fusion.1
  657.3 1.3 broadcast_divide_fusion.2
  658.6 1.3 broadcast_divide_fusion.3
  (63 shorter events, 2.8 us)
Async XLA Ops:
  7.2 239.3 %copy-start = (bf16[200,800]{1,0:T(8,128)(2,1)S(1)}, bf16[200,800]{1,0:T(8,128)(2,1)}, u32[]{:S(2)}) copy-start(bf16[200,800]{1,0:T(8,128)(2,1)} %param.15) | copy-start | bytes 960004
  7.2 18.8 %copy-start.10 = (f32[200,49]{0,1:T(8,128)S(1)}, f32[200,49]{0,1:T(8,128)}, u32[]{:S(2)}) copy-start(f32[200,49]{0,1:T(8,128)} %param.13) | copy-start | bytes 117604
  7.2 37.7 %copy-start.9 = (bf16[77,200]{1,0:T(8,128)(2,1)S(1)}, bf16[77,200]{1,0:T(8,128)(2,1)}, u32[]{:S(2)}) copy-start(bf16[77,200]{1,0:T(8,128)(2,1)} %param.12) | copy-start | bytes 92404
  9.6 11.9 %all-to-all-start = ((s32[16,1,2]{2,1,0:T(1,128)}), s32[16,1,2]{2,1,0:T(1,128)S(1)}, u32[]{:S(2)}, u32[]{:S(2)}) async-start(s32[16,1,2]{2,1,0:T(1,128)} %bitcast.9), calls=%async_computation | async-start | bytes 16384 | tf_op jit(solution)/shard_map/all_to_all | solution.py:84
  21.4 23.2 %all-to-all-start.1 = ((bf16[16,2,77,256]{3,1,2,0:T(2,128)(2,1)}), bf16[16,2,77,256]{3,1,2,0:T(2,128)(2,1)S(1)}, u32[]{:S(2)}, u32[]{:S(2)}) async-start(bf16[16,2,77,256]{3,1,2,0:T(2,128)(2,1)} %copy.69), calls=%async_computation.1 | async-start | bytes 2523136 | tf_op jit(solution)/shard_map/all_to_all | solution.py:83
  58.7 23.4 %copy-start.6 = (bf16[200,4,16,8,16]{0,4,3,2,1:T(8,128)(2,1)}, bf16[200,4,16,8,16]{0,4,3,2,1:T(8,128)(2,1)S(1)}, u32[]{:S(2)}) copy-start(bf16[200,4,16,8,16]{0,4,3,2,1:T(8,128)(2,1)S(1)} %copy.73) | copy-start | bytes 9830404
  58.8 9.3 %collective-permute-start = (bf16[200,64,3]{0,2,1:T(4,128)(2,1)S(1)}, bf16[200,64,3]{0,2,1:T(4,128)(2,1)S(1)}, u32[]{:S(2)}, u32[]{:S(2)}) collective-permute-start(bf16[200,64,3]{0,2,1:T(4,128)(2,1)S(1)} %get-tuple-element.85), channel_id=1, source_target_pairs={{0,1},{1,2},{2,3},{3,4},{4,5},{5,6},{6,7},{7,0},{8,9},{9,10},{10,1... | collective-permute-start | bytes 230408 | tf_op jit(solution)/shard_map/ppermute | solution.py:23
  60.5 7.7 %collective-permute-start.1 = (bf16[200,64,3]{0,2,1:T(4,128)(2,1)S(1)}, bf16[200,64,3]{0,2,1:T(4,128)(2,1)S(1)}, u32[]{:S(2)}, u32[]{:S(2)}) collective-permute-start(bf16[200,64,3]{0,2,1:T(4,128)(2,1)S(1)} %get-tuple-element.86), channel_id=1, source_target_pairs={{1,0},{2,1},{3,2},{4,3},{5,4},{6,5},{7,6},{0,7},{9,8},{10,9},{11,1... | collective-permute-start | bytes 230408 | tf_op jit(solution)/shard_map/ppermute | solution.py:26
  68.2 2.8 collective-permute-start.2
  69.5 4.4 collective-permute-start.3
  82.0 68.1 %copy-start.2 = (bf16[200,67,134]{0,2,1:T(8,128)(2,1)}, bf16[200,67,134]{0,2,1:T(8,128)(2,1)S(1)}, u32[]{:S(2)}) copy-start(bf16[200,67,134]{0,2,1:T(8,128)(2,1)S(1)} %get-tuple-element.81) | copy-start | bytes 10773604
  82.0 68.1 %copy-start.3 = (bf16[200,67,134]{0,2,1:T(8,128)(2,1)}, bf16[200,67,134]{0,2,1:T(8,128)(2,1)S(1)}, u32[]{:S(2)}) copy-start(bf16[200,67,134]{0,2,1:T(8,128)(2,1)S(1)} %get-tuple-element.82) | copy-start | bytes 10773604
  150.2 5.1 copy-start.4
  150.2 2.5 copy-start.11
  236.1 11.0 %copy-start.13 = (bf16[800,200]{0,1:T(8,128)(2,1)S(1)}, bf16[800,200]{0,1:T(8,128)(2,1)}, u32[]{:S(2)}) copy-start(bf16[800,200]{0,1:T(8,128)(2,1)} %param.16) | copy-start | bytes 960004
  247.1 3.7 copy-start.8
  267.7 111.4 %all-to-all-start.3 = ((bf16[16,2,200,256]{3,1,2,0:T(2,128)(2,1)}), bf16[16,2,200,256]{3,1,2,0:T(2,128)(2,1)}, u32[]{:S(2)}, u32[]{:S(2)}) async-start(bf16[16,2,200,256]{3,1,2,0:T(2,128)(2,1)} %copy.82), calls=%async_computation.3 | async-start | bytes 6553600 | tf_op jit(solution)/shard_map/all_to_all | solution.py:129
  272.4 5.9 copy-start.12
  272.4 106.7 %all-reduce.9.cloned.1.call-start = ((), (), s32[]{:S(2)}) async-start(), calls=%async_computation.5 | async-start | bytes 2867200 | tf_op jit(solution)/shard_map/psum | solution.py:149
  278.2 373.7 %all-reduce.7.cloned.1.call-start = ((), (), s32[]{:S(2)}) async-start(), calls=%async_computation.4 | async-start | bytes 2867200 | tf_op jit(solution)/shard_map/psum | solution.py:149
  418.6 8.8 %copy-start.7 = (f32[200,4,16,8,16]{0,4,3,2,1:T(8,128)}, f32[200,4,16,8,16]{0,4,3,2,1:T(8,128)S(1)}, u32[]{:S(2)}) copy-start(f32[200,4,16,8,16]{0,4,3,2,1:T(8,128)S(1)} %copy.85) | copy-start | bytes 19660804
  427.4 127.9 %slice-start = ((s8[4665344]{0:T(1024)(128)(4,1)}), s8[471040]{0:T(1024)(128)(4,1)S(1)}, s32[]{:S(2)}) async-start(s8[4665344]{0:T(1024)(128)(4,1)} %bitcast.224), calls=%async_computation.6 | async-start | bytes 942080
  478.0 77.3 %slice-start.1 = ((s8[4665344]{0:T(1024)(128)(4,1)}), s8[4194304]{0:T(1024)(128)(4,1)S(1)}, s32[]{:S(2)}) async-start(s8[4665344]{0:T(1024)(128)(4,1)} %bitcast.224), calls=%async_computation.7 | async-start | bytes 8388608
  527.8 27.6 %copy-start.5 = (f32[200,64,128]{0,2,1:T(8,128)S(1)}, f32[200,64,128]{0,2,1:T(8,128)}, u32[]{:S(2)}) copy-start(f32[200,64,128]{0,2,1:T(8,128)} %get-tuple-element.76) | copy-start | bytes 19660804
  527.8 132.1 %copy-start.1 = (bf16[200,800]{1,0:T(8,128)(2,1)S(1)}, bf16[200,800]{1,0:T(8,128)(2,1)}, u32[]{:S(2)}) copy-start(bf16[200,800]{1,0:T(8,128)(2,1)} %param.15) | copy-start | bytes 960004
Sparse Core Ops, SparseCore 0:
  278.3 100.6 all-reduce.8
  381.6 119.8 all-reduce.6
